TPU v7x, 32 devices: a whole 2x2x4 slice. The times are simulated.
32 devices in a mesh: wide: 16 (over z, x, core), narrow: 2 (over y).
Axes of the slice: x: 2, y: 2, z: 4, core: 2. Of those that a mesh axis runs over, the one named last changes fastest.
Arguments:
- embeddings: float32 [16384, 512], P(('wide', 'narrow')), may hold values from -2.1 to 2.1
- accum: float32 [16384], P(('wide', 'narrow')), may hold values from 0.01 to 1
- relation: bfloat16 [512, 512], replicated, may hold values from -0.25 to 0.25
- head_index: int32 [2, 16384], P(None, ('wide', 'narrow')), may hold values from 0 to 511
- tail_index: int32 [2, 16384], P(None, ('wide', 'narrow')), may hold values from 0 to 511
- negative_index: int32 [2, 8192], P(None, ('wide', 'narrow')), may hold values from 0 to 511
- partner: int32 [2, 16], replicated, may hold values from 0 to 15, each once within a row
- edge_count: int32 [2, 32], P(None, ('wide', 'narrow')), may hold values from 1 to 512, 8192 in all within a row
Outputs:
- new_embeddings: float32 [16384, 512], P(('wide', 'narrow'))
- new_accum: float32 [16384], P(('wide', 'narrow'))
- relation_grad: float32 [512, 512], replicated
- edge_losses: float32 [2, 16384], P(None, ('wide', 'narrow'))
Inputs may be any that keep to these rules, and one draw needn't show every extreme that they name: Each row of partner is a permutation of the wide indices. `edge_count`: in each bucket step the counts of all devices sum to half of all slots, and some device has exactly 512.
All inputs are finite; a program needn't handle non-finite values.
Results may differ from a plain program's by a relative error of at most 0.0064.
Values may be sent and summed in bfloat16 or wider, within the bound.
A program may use at most 64 MiB of HBM per device.

v0:
```python
import jax
import jax.numpy as jnp
from jax import lax
from jax.sharding import PartitionSpec as P

LEARN_RATE = 0.1
EPSILON = 1e-06


def as_sent(array):

    def short(part):
        return part.astype(jnp.bfloat16) if part.dtype == jnp.float32 else part

    return jax.tree.map(short, array)


def split_rows(values, parts):
    return values.reshape((parts, values.shape[0] // parts) + values.shape[1:])


def join_rows(values):
    return values.reshape((values.shape[0] * values.shape[1],) + values.shape[2:])


def invert(order):
    positions = jnp.arange(order.shape[0], dtype=jnp.int32)
    return jnp.sum(jnp.where(order[:, None] == positions[None, :], positions[:, None], 0), axis=0)


def bucket_terms(query_bf, tail_ids, block_bf, neg_ids):
    tail_rows = jnp.take(block_bf, tail_ids, axis=0)
    own_negs = jnp.take(block_bf, neg_ids, axis=0)
    negatives = lax.all_gather(own_negs, "narrow", axis=0, tiled=True)
    positive = jnp.sum(query_bf.astype(jnp.float32) * tail_rows.astype(jnp.float32), axis=1)
    scores = lax.dot_general(
        query_bf, negatives, (((1,), (1,)), ((), ())), preferred_element_type=jnp.float32
    )
    exp_pos = jnp.exp(positive)
    exp_neg = jnp.exp(scores)
    total = exp_pos + jnp.sum(exp_neg, axis=1)
    losses = jnp.log(total) - positive
    pos_weight = exp_pos / total - 1.0
    weights = (exp_neg / total[:, None]).astype(jnp.bfloat16)
    query_grad = pos_weight[:, None] * tail_rows.astype(jnp.float32) + jnp.dot(
        weights, negatives, preferred_element_type=jnp.float32
    )
    tail_pos = pos_weight[:, None] * query_bf.astype(jnp.float32)
    negative_grad = lax.psum_scatter(
        lax.dot_general(
            weights, query_bf, (((0,), (0,)), ((), ())), preferred_element_type=jnp.float32
        ).astype(jnp.bfloat16),
        "narrow",
        scatter_dimension=0,
        tiled=True,
    ).astype(jnp.float32)
    tail_grad = (
        jnp.zeros(block_bf.shape, jnp.float32)
        .at[tail_ids]
        .add(tail_pos)
        .at[neg_ids]
        .add(negative_grad)
    )
    return (losses, query_grad, tail_grad)


def on_device(
    embeddings, accum, relation, head_index, tail_index, negative_index, partner, edge_count
):
    wide_size = lax.axis_size("wide")
    step_total = head_index.shape[0]
    positions = jnp.arange(head_index.shape[1], dtype=jnp.int32)
    relation_sum = jnp.zeros(relation.shape, jnp.float32)
    loss_rows = []
    for step in range(step_total):
        order = partner[step]
        inverse = invert(order)
        live = positions < edge_count[step, 0]
        block_bf = embeddings.astype(jnp.bfloat16)
        head_rows = jnp.take(block_bf, head_index[step], axis=0)
        query = jnp.dot(head_rows, relation, preferred_element_type=jnp.float32)
        query_bf = jnp.where(live[:, None], query, 0.0).astype(jnp.bfloat16)
        outgoing = lax.all_to_all(
            split_rows(block_bf, wide_size), "wide", split_axis=0, concat_axis=0, tiled=True
        )
        incoming = lax.all_to_all(
            jnp.take(outgoing, order, axis=0), "wide", split_axis=0, concat_axis=0, tiled=True
        )
        losses, query_grad, tail_grad = bucket_terms(
            query_bf, tail_index[step], join_rows(incoming), negative_index[step]
        )
        sent = lax.all_to_all(
            split_rows(tail_grad, wide_size).astype(jnp.bfloat16),
            "wide",
            split_axis=0,
            concat_axis=0,
            tiled=True,
        ).astype(jnp.float32)
        back = lax.all_to_all(
            as_sent(jnp.take(sent, inverse, axis=0)),
            "wide",
            split_axis=0,
            concat_axis=0,
            tiled=True,
        )
        owner_grad = join_rows(back)
        grad_bf = jnp.where(live[:, None], query_grad, 0.0).astype(jnp.bfloat16)
        head_term = lax.dot_general(
            grad_bf, relation, (((1,), (1,)), ((), ())), preferred_element_type=jnp.float32
        )
        head_grad = jnp.zeros(embeddings.shape, jnp.float32).at[head_index[step]].add(head_term)
        relation_part = lax.dot_general(
            head_rows, grad_bf, (((0,), (0,)), ((), ())), preferred_element_type=jnp.float32
        )
        relation_sum = relation_sum + relation_part
        grads = head_grad + owner_grad
        accum = accum + jnp.mean(grads * grads, axis=1)
        embeddings = embeddings - LEARN_RATE * grads / (jnp.sqrt(accum)[:, None] + EPSILON)
        loss_rows.append(jnp.where(live, losses, 0.0))
    relation_sum = lax.psum(relation_sum, ("wide", "narrow"))
    return (embeddings, accum, relation_sum, jnp.stack(loss_rows))


def solution(mesh):
    in_specs = (
        P(("wide", "narrow"), None),
        P(("wide", "narrow")),
        P(),
        P(None, ("wide", "narrow")),
        P(None, ("wide", "narrow")),
        P(None, ("wide", "narrow")),
        P(),
        P(None, ("wide", "narrow")),
    )
    out_specs = (
        P(("wide", "narrow"), None),
        P(("wide", "narrow")),
        P(),
        P(None, ("wide", "narrow")),
    )
    return jax.shard_map(
        on_device, mesh=mesh, in_specs=in_specs, out_specs=out_specs, check_vma=False
    )
```

profile of v0, /device:TPU:0, one launch (start us, length us, event | category | flops | bytes accessed | tf_op | source)
XLA Modules:
  0.0 378.0 jit_solution(17429168418496107216)
XLA Ops:
  9.3 7.5 %all-to-all-start = ((bf16[16,32,512]{2,1,0:T(8,128)(2,1)}), bf16[16,32,512]{2,1,0:T(8,128)(2,1)S(1)}, u32[]{:S(2)}, u32[]{:S(2)}) async-start(bf16[16,32,512]{2,1,0:T(8,128)(2,1)} %bitcast.6), calls=%async_computation | async-start | bytes 1048576 | tf_op jit(solution)/shard_map/all_to_all | solution.py:83
  21.4 9.7 %all-to-all-done = bf16[16,32,512]{2,1,0:T(8,128)(2,1)S(1)} async-done(((bf16[16,32,512]{2,1,0:T(8,128)(2,1)}), bf16[16,32,512]{2,1,0:T(8,128)(2,1)S(1)}, u32[]{:S(2)}, u32[]{:S(2)}) %all-to-all-start) | async-done | bytes 524320 | tf_op jit(solution)/shard_map/all_to_all | solution.py:83
  32.6 4.2 %all-to-all-start.1 = ((bf16[16,32,512]{2,1,0:T(8,128)(2,1)}), bf16[16,32,512]{2,1,0:T(8,128)(2,1)S(1)}, u32[]{:S(2)}, u32[]{:S(2)}) async-start(bf16[16,32,512]{2,1,0:T(8,128)(2,1)} %broadcast_select_fusion.2), calls=%async_computation.1 | async-start | bytes 1048576 | tf_op jit(solution)/shard_map/all_to_all | solution.py:86
  38.8 12.3 %all-to-all-done.1 = bf16[16,32,512]{2,1,0:T(8,128)(2,1)S(1)} async-done(((bf16[16,32,512]{2,1,0:T(8,128)(2,1)}), bf16[16,32,512]{2,1,0:T(8,128)(2,1)S(1)}, u32[]{:S(2)}, u32[]{:S(2)}) %all-to-all-start.1) | async-done | bytes 524320 | tf_op jit(solution)/shard_map/all_to_all | solution.py:86
  54.5 9.0 %all_gather.6 = bf16[512,512]{1,0:T(8,128)(2,1)S(1)} all-gather(bf16[256,512]{1,0:T(8,128)(2,1)S(1)} %broadcast_select_fusion.7), channel_id=1, replica_groups=mesh['wide'=16,'narrow'=2] {'narrow'}, dimensions={0}, use_global_device_ids=true | all-gather | bytes 786432 | tf_op jit(solution)/shard_map/all_gather | solution.py:34
  68.4 4.5 %scatter_custom_fusion = f32[512,512]{1,0:T(8,128)S(1)} fusion(s32[512]{0:T(512)S(1)} %bitcast.92, f32[512,512]{1,0:T(8,128)} %copy.30, f32[]{:T(128)} %constant.39.clone.1), kind=kCustom, calls=%fused_computation.49 | custom fusion | flops 262144 | bytes 1049088 | tf_op jit(solution)/shard_map/scatter-add | solution.py:60
  72.9 8.6 %reduce-scatter.3.cloned.1.call-done = bf16[256,512]{1,0:T(8,128)(2,1)} async-done(((bf16[512,512]{1,0:T(8,128)(2,1)}), bf16[256,512]{1,0:T(8,128)(2,1)}) %reduce-scatter.3.cloned.1.call-update) | async-done | bytes 262160 | tf_op jit(solution)/shard_map/reduce_scatter | solution.py:49
  85.2 5.6 %all-to-all-start.2 = ((bf16[16,32,512]{2,1,0:T(8,128)(2,1)}), bf16[16,32,512]{2,1,0:T(8,128)(2,1)S(1)}, u32[]{:S(2)}, u32[]{:S(2)}) async-start(bf16[16,32,512]{2,1,0:T(8,128)(2,1)} %bitcast.11), calls=%async_computation.3 | async-start | bytes 1048576 | tf_op jit(solution)/shard_map/all_to_all | solution.py:92
  91.0 14.1 %all-to-all-done.2 = bf16[16,32,512]{2,1,0:T(8,128)(2,1)S(1)} async-done(((bf16[16,32,512]{2,1,0:T(8,128)(2,1)}), bf16[16,32,512]{2,1,0:T(8,128)(2,1)S(1)}, u32[]{:S(2)}, u32[]{:S(2)}) %all-to-all-start.2) | async-done | bytes 524320 | tf_op jit(solution)/shard_map/all_to_all | solution.py:92
  106.7 4.4 %all-to-all-start.3 = ((bf16[16,32,512]{2,1,0:T(8,128)(2,1)}), bf16[16,32,512]{2,1,0:T(8,128)(2,1)}, u32[]{:S(2)}, u32[]{:S(2)}) async-start(bf16[16,32,512]{2,1,0:T(8,128)(2,1)} %select_convert_fusion.1), calls=%async_computation.4 | async-start | bytes 1048576 | tf_op jit(solution)/shard_map/all_to_all | solution.py:99
  113.4 11.9 %all-to-all-done.3 = bf16[16,32,512]{2,1,0:T(8,128)(2,1)} async-done(((bf16[16,32,512]{2,1,0:T(8,128)(2,1)}), bf16[16,32,512]{2,1,0:T(8,128)(2,1)}, u32[]{:S(2)}, u32[]{:S(2)}) %all-to-all-start.3) | async-done | bytes 524320 | tf_op jit(solution)/shard_map/all_to_all | solution.py:99
  126.5 4.2 %scatter_fusion = f32[512,512]{1,0:T(8,128)S(1)} fusion(f32[512,512]{1,0:T(8,128)S(1)} %bitcast_convert_fusion.1, s32[512]{0:T(512)S(1)} %bitcast.84, f32[512,512]{1,0:T(8,128)S(1)} %fusion.28), kind=kCustom, calls=%fused_computation.12 | custom fusion | flops 262144 | bytes 3147776 | tf_op jit(solution)/shard_map/scatter-add | solution.py:111
  133.0 4.2 %all-to-all-start.4 = ((bf16[16,32,512]{2,1,0:T(8,128)(2,1)}), bf16[16,32,512]{2,1,0:T(8,128)(2,1)S(1)}, u32[]{:S(2)}, u32[]{:S(2)}) async-start(bf16[16,32,512]{2,1,0:T(8,128)(2,1)} %bitcast.21), calls=%async_computation.5 | async-start | bytes 1048576 | tf_op jit(solution)/shard_map/all_to_all | solution.py:83
  137.2 14.2 %all-to-all-done.4 = bf16[16,32,512]{2,1,0:T(8,128)(2,1)S(1)} async-done(((bf16[16,32,512]{2,1,0:T(8,128)(2,1)}), bf16[16,32,512]{2,1,0:T(8,128)(2,1)S(1)}, u32[]{:S(2)}, u32[]{:S(2)}) %all-to-all-start.4) | async-done | bytes 524320 | tf_op jit(solution)/shard_map/all_to_all | solution.py:83
  161.6 9.7 %all-to-all-done.5 = bf16[16,32,512]{2,1,0:T(8,128)(2,1)S(1)} async-done(((bf16[16,32,512]{2,1,0:T(8,128)(2,1)}), bf16[16,32,512]{2,1,0:T(8,128)(2,1)S(1)}, u32[]{:S(2)}, u32[]{:S(2)}) %all-to-all-start.5) | async-done | bytes 524320 | tf_op jit(solution)/shard_map/all_to_all | solution.py:86
  174.9 9.2 %all_gather.7 = bf16[512,512]{1,0:T(8,128)(2,1)S(1)} all-gather(bf16[256,512]{1,0:T(8,128)(2,1)S(1)} %broadcast_select_fusion.6), channel_id=1, replica_groups=mesh['wide'=16,'narrow'=2] {'narrow'}, dimensions={0}, use_global_device_ids=true | all-gather | bytes 786432 | tf_op jit(solution)/shard_map/all_gather | solution.py:34
  190.2 4.5 %scatter_custom_fusion.3 = f32[512,512]{1,0:T(8,128)S(1)} fusion(s32[512]{0:T(512)S(1)} %bitcast.91, f32[512,512]{1,0:T(8,128)} %copy.34, f32[]{:T(128)} %constant.39.clone.1), kind=kCustom, calls=%fused_computation.47 | custom fusion | flops 262144 | bytes 1049088 | tf_op jit(solution)/shard_map/scatter-add | solution.py:60
  194.7 6.5 %reduce-scatter.5.cloned.1.call-done = bf16[256,512]{1,0:T(8,128)(2,1)} async-done(((bf16[512,512]{1,0:T(8,128)(2,1)}), bf16[256,512]{1,0:T(8,128)(2,1)}) %reduce-scatter.5.cloned.1.call-update) | async-done | bytes 262160 | tf_op jit(solution)/shard_map/reduce_scatter | solution.py:49
  205.2 5.7 %all-to-all-start.6 = ((bf16[16,32,512]{2,1,0:T(8,128)(2,1)}), bf16[16,32,512]{2,1,0:T(8,128)(2,1)}, u32[]{:S(2)}, u32[]{:S(2)}) async-start(bf16[16,32,512]{2,1,0:T(8,128)(2,1)} %bitcast.72), calls=%async_computation.8 | async-start | bytes 1048576 | tf_op jit(solution)/shard_map/all_to_all | solution.py:92
  213.3 11.9 %all-to-all-done.6 = bf16[16,32,512]{2,1,0:T(8,128)(2,1)} async-done(((bf16[16,32,512]{2,1,0:T(8,128)(2,1)}), bf16[16,32,512]{2,1,0:T(8,128)(2,1)}, u32[]{:S(2)}, u32[]{:S(2)}) %all-to-all-start.6) | async-done | bytes 524320 | tf_op jit(solution)/shard_map/all_to_all | solution.py:92
  227.8 4.4 %all-to-all-start.7 = ((bf16[16,32,512]{2,1,0:T(8,128)(2,1)}), bf16[16,32,512]{2,1,0:T(8,128)(2,1)}, u32[]{:S(2)}, u32[]{:S(2)}) async-start(bf16[16,32,512]{2,1,0:T(8,128)(2,1)} %select_convert_fusion), calls=%async_computation.9 | async-start | bytes 1048576 | tf_op jit(solution)/shard_map/all_to_all | solution.py:99
  239.4 7.1 %all-to-all-done.7 = bf16[16,32,512]{2,1,0:T(8,128)(2,1)} async-done(((bf16[16,32,512]{2,1,0:T(8,128)(2,1)}), bf16[16,32,512]{2,1,0:T(8,128)(2,1)}, u32[]{:S(2)}, u32[]{:S(2)}) %all-to-all-start.7) | async-done | bytes 524320 | tf_op jit(solution)/shard_map/all_to_all | solution.py:99
  247.7 4.7 %scatter_fusion.1 = f32[512,512]{1,0:T(8,128)S(1)} fusion(f32[512,512]{1,0:T(8,128)S(1)} %bitcast_convert_fusion, s32[512]{0:T(512)S(1)} %bitcast.83, f32[512,512]{1,0:T(8,128)} %fusion.29), kind=kCustom, calls=%fused_computation.15 | custom fusion | flops 262144 | bytes 3147776 | tf_op jit(solution)/shard_map/scatter-add | solution.py:111
  255.0 114.2 %all-reduce.2.cloned.1.call-done = f32[512,512]{1,0:T(8,128)} async-done(((f32[512,512]{1,0:T(8,128)}), f32[512,512]{1,0:T(8,128)}) %all-reduce.2.cloned.1.call-update) | async-done | bytes 1048592 | tf_op jit(solution)/shard_map/psum | solution.py:120
  (141 shorter events, 71.4 us)
Async XLA Ops:
  7.2 56.4 %copy-start = (bf16[512,512]{1,0:T(8,128)(2,1)S(1)}, bf16[512,512]{1,0:T(8,128)(2,1)}, u32[]{:S(2)}) copy-start(bf16[512,512]{1,0:T(8,128)(2,1)} %param.18) | copy-start | bytes 1572868
  9.3 7.5 %copy-start.20 = (s32[2,16]{1,0:T(2,128)S(1)}, s32[2,16]{1,0:T(2,128)}, u32[]{:S(2)}) copy-start(s32[2,16]{1,0:T(2,128)} %param.22) | copy-start | bytes 388
  9.3 7.6 %copy-start.17 = (s32[2,512]{1,0:T(2,128)S(1)}, s32[2,512]{1,0:T(2,128)}, u32[]{:S(2)}) copy-start(s32[2,512]{1,0:T(2,128)} %param.19) | copy-start | bytes 12292
  9.3 21.8 %all-to-all-start = ((bf16[16,32,512]{2,1,0:T(8,128)(2,1)}), bf16[16,32,512]{2,1,0:T(8,128)(2,1)S(1)}, u32[]{:S(2)}, u32[]{:S(2)}) async-start(bf16[16,32,512]{2,1,0:T(8,128)(2,1)} %bitcast.6), calls=%async_computation | async-start | bytes 1048576 | tf_op jit(solution)/shard_map/all_to_all | solution.py:83
  32.6 18.4 %all-to-all-start.1 = ((bf16[16,32,512]{2,1,0:T(8,128)(2,1)}), bf16[16,32,512]{2,1,0:T(8,128)(2,1)S(1)}, u32[]{:S(2)}, u32[]{:S(2)}) async-start(bf16[16,32,512]{2,1,0:T(8,128)(2,1)} %broadcast_select_fusion.2), calls=%async_computation.1 | async-start | bytes 1048576 | tf_op jit(solution)/shard_map/all_to_all | solution.py:86
  36.8 44.7 %reduce-scatter.3.cloned.1.call-start = ((), (), s32[]{:S(2)}) async-start(), calls=%async_computation.10 | async-start | bytes 786432 | tf_op jit(solution)/shard_map/reduce_scatter | solution.py:49
  54.4 9.1 %copy-start.15 = (bf16[512,512]{0,1:T(8,128)(2,1)}, bf16[512,512]{0,1:T(8,128)(2,1)S(1)}, u32[]{:S(2)}) copy-start(bf16[512,512]{0,1:T(8,128)(2,1)S(1)} %copy.28) | copy-start | bytes 1572868
  64.6 1.0 copy-start.12
  85.2 19.9 %all-to-all-start.2 = ((bf16[16,32,512]{2,1,0:T(8,128)(2,1)}), bf16[16,32,512]{2,1,0:T(8,128)(2,1)S(1)}, u32[]{:S(2)}, u32[]{:S(2)}) async-start(bf16[16,32,512]{2,1,0:T(8,128)(2,1)} %bitcast.11), calls=%async_computation.3 | async-start | bytes 1048576 | tf_op jit(solution)/shard_map/all_to_all | solution.py:92
  106.7 4.4 %copy-start.13 = (f32[512,512]{0,1:T(8,128)S(1)}, f32[512,512]{0,1:T(8,128)}, u32[]{:S(2)}) copy-start(f32[512,512]{0,1:T(8,128)} %copy-done.12) | copy-start | bytes 3145732
  106.7 18.7 %all-to-all-start.3 = ((bf16[16,32,512]{2,1,0:T(8,128)(2,1)}), bf16[16,32,512]{2,1,0:T(8,128)(2,1)}, u32[]{:S(2)}, u32[]{:S(2)}) async-start(bf16[16,32,512]{2,1,0:T(8,128)(2,1)} %select_convert_fusion.1), calls=%async_computation.4 | async-start | bytes 1048576 | tf_op jit(solution)/shard_map/all_to_all | solution.py:99
  130.7 1.2 copy-start.1
  133.0 18.4 %all-to-all-start.4 = ((bf16[16,32,512]{2,1,0:T(8,128)(2,1)}), bf16[16,32,512]{2,1,0:T(8,128)(2,1)S(1)}, u32[]{:S(2)}, u32[]{:S(2)}) async-start(bf16[16,32,512]{2,1,0:T(8,128)(2,1)} %bitcast.21), calls=%async_computation.5 | async-start | bytes 1048576 | tf_op jit(solution)/shard_map/all_to_all | solution.py:83
  152.9 18.4 %all-to-all-start.5 = ((bf16[16,32,512]{2,1,0:T(8,128)(2,1)}), bf16[16,32,512]{2,1,0:T(8,128)(2,1)S(1)}, u32[]{:S(2)}, u32[]{:S(2)}) async-start(bf16[16,32,512]{2,1,0:T(8,128)(2,1)} %broadcast_select_fusion), calls=%async_computation.6 | async-start | bytes 1048576 | tf_op jit(solution)/shard_map/all_to_all | solution.py:86
  157.1 44.1 %reduce-scatter.5.cloned.1.call-start = ((), (), s32[]{:S(2)}) async-start(), calls=%async_computation.11 | async-start | bytes 786432 | tf_op jit(solution)/shard_map/reduce_scatter | solution.py:49
  174.7 9.3 %copy-start.14 = (bf16[512,512]{0,1:T(8,128)(2,1)}, bf16[512,512]{0,1:T(8,128)(2,1)S(1)}, u32[]{:S(2)}) copy-start(bf16[512,512]{0,1:T(8,128)(2,1)S(1)} %copy.32) | copy-start | bytes 1572868
  174.8 9.2 %copy-start.7 = (bf16[512,512]{1,0:T(8,128)(2,1)S(1)}, bf16[512,512]{1,0:T(8,128)(2,1)}, u32[]{:S(2)}) copy-start(bf16[512,512]{1,0:T(8,128)(2,1)} %gather_fusion.5) | copy-start | bytes 1572868
  205.2 20.0 %all-to-all-start.6 = ((bf16[16,32,512]{2,1,0:T(8,128)(2,1)}), bf16[16,32,512]{2,1,0:T(8,128)(2,1)}, u32[]{:S(2)}, u32[]{:S(2)}) async-start(bf16[16,32,512]{2,1,0:T(8,128)(2,1)} %bitcast.72), calls=%async_computation.8 | async-start | bytes 1048576 | tf_op jit(solution)/shard_map/all_to_all | solution.py:92
  227.8 4.4 %copy-start.4 = (bf16[512,512]{1,0:T(8,128)(2,1)S(1)}, bf16[512,512]{1,0:T(8,128)(2,1)}, u32[]{:S(2)}) copy-start(bf16[512,512]{1,0:T(8,128)(2,1)} %copy-done.3) | copy-start | bytes 1572868
  227.8 18.8 %all-to-all-start.7 = ((bf16[16,32,512]{2,1,0:T(8,128)(2,1)}), bf16[16,32,512]{2,1,0:T(8,128)(2,1)}, u32[]{:S(2)}, u32[]{:S(2)}) async-start(bf16[16,32,512]{2,1,0:T(8,128)(2,1)} %select_convert_fusion), calls=%async_computation.9 | async-start | bytes 1048576 | tf_op jit(solution)/shard_map/all_to_all | solution.py:99
  232.2 137.1 %all-reduce.2.cloned.1.call-start = ((), (), s32[]{:S(2)}) async-start(), calls=%async_computation.12 | async-start | bytes 2097152 | tf_op jit(solution)/shard_map/psum | solution.py:120
  232.2 2.7 copy-start.8
  236.6 1.4 copy-start.10
  252.4 1.2 copy-start.2
  (9 other events, 6.9 us)
Sparse Core Ops, SparseCore 0:
  67.0 14.3 reduce-scatter.2
  187.7 13.4 reduce-scatter.4
  238.2 131.0 all-reduce.1
where the time goes:
time: 380 us; the launch traced here: 378 us
  waiting for transfers between devices  220 us (58%)
  other arithmetic  42.3 us (11%)
  starting transfers between devices  40.2 us (11%)
  local copies, waits for them, and re-layouts  29.1 us (8%)
  blocking collectives  18.2 us (5%)
  between operations  14.4 us (4%)
  matrix products  13.4 us (4%)
    psum x1, waiting for transfers between devices, on_device(): relation_sum = lax.psum(relation_sum, ('wide', 'narrow'))  114 us
    all_to_all x2, waiting for transfers between devices, on_device(): lax.all_to_all(split_rows(tail_grad, wide_size).astype(jnp.bfloat16), 'wi...  26.1 us
    all_to_all x2, waiting for transfers between devices, on_device(): lax.all_to_all(split_rows(block_bf, wide_size), 'wide', split_axis=0, con...  23.9 us
    all_to_all x2, waiting for transfers between devices, on_device(): lax.all_to_all(jnp.take(outgoing, order, axis=0), 'wide', split_axis=0, c...  22 us
    all_to_all x2, waiting for transfers between devices, on_device(): lax.all_to_all(as_sent(jnp.take(sent, inverse, axis=0)), 'wide', split_ax...  19.1 us
    all_gather x2, blocking collectives, bucket_terms(): negatives = lax.all_gather(own_negs, 'narrow', axis=0, tiled=True)  18.2 us
    scatter-add x4, other arithmetic, bucket_terms(): tail_grad = jnp.zeros(block_bf.shape, jnp.float32).at[tail_ids].add(tail_...  15.1 us
    reduce_scatter x2, waiting for transfers between devices, bucket_terms(): lax.psum_scatter(lax.dot_general(weights, query_bf, (((0,), (0,)), ((), (...  15.1 us
  transfers between devices with their start and end apart: 11, of which 11 were waited for; matrix products, arithmetic and copies ran while one was open for 11% of the time, Pallas kernels for 0%

commit v1 on v0

--- a/solution.py
+++ b/solution.py
@@ -117,7 +117,7 @@
         accum = accum + jnp.mean(grads * grads, axis=1)
         embeddings = embeddings - LEARN_RATE * grads / (jnp.sqrt(accum)[:, None] + EPSILON)
         loss_rows.append(jnp.where(live, losses, 0.0))
-    relation_sum = lax.psum(relation_sum, ("wide", "narrow"))
+    relation_sum = jnp.sum(lax.all_gather(relation_sum, ("wide", "narrow")), axis=0)
     return (embeddings, accum, relation_sum, jnp.stack(loss_rows))
 
 

time: 380 us -> 435 us (1.14)
  waiting for transfers between devices: 220 us -> 250 us
  other arithmetic: 42.3 us -> 59.4 us
  starting transfers between devices: 40.2 us -> 46.2 us
  matrix products: 13.4 us -> 19.3 us
    all_gather x0 -> x1, waiting for transfers between devices: none -> 144 us  [on_device(): lax.all_gather(relation_sum, ('wide', 'narrow'))]
    psum x1 -> x0, waiting for transfers between devices: 114 us -> none  [on_device(): relation_sum = lax.psum(relation_sum, ('wide', 'narrow'))]
    reduce_sum x0 -> x1, other arithmetic: none -> 13.2 us  [on_device(): jnp.sum(lax.all_gather(relation_sum, ('wide', 'narrow')), axis=0)]
    reduce_scatter x2, waiting for transfers between devices: 15.1 us -> 6.01 us  [bucket_terms(): lax.psum_scatter(lax.dot_general(weights, query_bf, (((0,), (0,)), ((), (...]
    all_to_all x2, waiting for transfers between devices: 26.1 us -> 34.4 us  [on_device(): lax.all_to_all(split_rows(tail_grad, wide_size).astype(jnp.bfloat16), 'wi...]
    all_to_all x2, starting transfers between devices: 8.76 us -> 15.5 us  [on_device(): lax.all_to_all(as_sent(jnp.take(sent, inverse, axis=0)), 'wide', split_ax...]
    unnamed x45 -> x24, local copies, waits for them, and re-layouts: 9.04 us -> 2.75 us
  transfers between devices with their start and end apart: 11 -> 11, of which waited for: 11 -> 10; matrix products, arithmetic and copies ran while one was open for 11% -> 13% of each run, Pallas kernels for 0% -> 0%
where the time goes in v1:
time: 435 us; the launch traced here: 433 us
  waiting for transfers between devices  250 us (57%)
  other arithmetic  59.4 us (14%)
  starting transfers between devices  46.2 us (11%)
  local copies, waits for them, and re-layouts  26.5 us (6%)
  matrix products  19.3 us (4%)
  blocking collectives  18 us (4%)
  between operations  14.3 us (3%)
    all_gather x1, waiting for transfers between devices, on_device(): lax.all_gather(relation_sum, ('wide', 'narrow'))  144 us
    all_to_all x2, waiting for transfers between devices, on_device(): lax.all_to_all(split_rows(tail_grad, wide_size).astype(jnp.bfloat16), 'wi...  34.4 us
    all_to_all x2, waiting for transfers between devices, on_device(): lax.all_to_all(split_rows(block_bf, wide_size), 'wide', split_axis=0, con...  22.2 us
    all_to_all x2, waiting for transfers between devices, on_device(): lax.all_to_all(jnp.take(outgoing, order, axis=0), 'wide', split_axis=0, c...  21.9 us
    all_to_all x2, waiting for transfers between devices, on_device(): lax.all_to_all(as_sent(jnp.take(sent, inverse, axis=0)), 'wide', split_ax...  20.6 us
    all_gather x2, blocking collectives, bucket_terms(): negatives = lax.all_gather(own_negs, 'narrow', axis=0, tiled=True)  18 us
    all_to_all x2, starting transfers between devices, on_device(): lax.all_to_all(as_sent(jnp.take(sent, inverse, axis=0)), 'wide', split_ax...  15.5 us
    scatter-add x4, other arithmetic, bucket_terms(): tail_grad = jnp.zeros(block_bf.shape, jnp.float32).at[tail_ids].add(tail_...  14.9 us
  transfers between devices with their start and end apart: 11, of which 10 were waited for; matrix products, arithmetic and copies ran while one was open for 13% of the time, Pallas kernels for 0%

profile of v1, /device:TPU:0, one launch (start us, length us, event | category | flops | bytes accessed | tf_op | source)
XLA Modules:
  0.0 433.3 jit_solution(2818424136673507374)
XLA Ops:
  9.3 7.4 %all-to-all-start = ((bf16[16,32,512]{2,1,0:T(8,128)(2,1)}), bf16[16,32,512]{2,1,0:T(8,128)(2,1)S(1)}, u32[]{:S(2)}, u32[]{:S(2)}) async-start(bf16[16,32,512]{2,1,0:T(8,128)(2,1)} %bitcast.6), calls=%async_computation | async-start | bytes 1048576 | tf_op jit(solution)/shard_map/all_to_all | solution.py:83
  23.0 8.0 %all-to-all-done = bf16[16,32,512]{2,1,0:T(8,128)(2,1)S(1)} async-done(((bf16[16,32,512]{2,1,0:T(8,128)(2,1)}), bf16[16,32,512]{2,1,0:T(8,128)(2,1)S(1)}, u32[]{:S(2)}, u32[]{:S(2)}) %all-to-all-start) | async-done | bytes 524320 | tf_op jit(solution)/shard_map/all_to_all | solution.py:83
  32.5 4.2 all-to-all-start.1
  38.7 12.2 %all-to-all-done.1 = bf16[16,32,512]{2,1,0:T(8,128)(2,1)S(1)} async-done(((bf16[16,32,512]{2,1,0:T(8,128)(2,1)}), bf16[16,32,512]{2,1,0:T(8,128)(2,1)S(1)}, u32[]{:S(2)}, u32[]{:S(2)}) %all-to-all-start.1) | async-done | bytes 524320 | tf_op jit(solution)/shard_map/all_to_all | solution.py:86
  55.2 9.0 %all_gather.12 = bf16[512,512]{1,0:T(8,128)(2,1)S(1)} all-gather(bf16[256,512]{1,0:T(8,128)(2,1)S(1)} %broadcast_select_fusion.7), channel_id=1, replica_groups=mesh['wide'=16,'narrow'=2] {'narrow'}, dimensions={0}, use_global_device_ids=true | all-gather | bytes 786432 | tf_op jit(solution)/shard_map/all_gather | solution.py:34
  72.9 4.5 %scatter_custom_fusion = f32[512,512]{1,0:T(8,128)S(1)} fusion(s32[512]{0:T(512)S(1)} %bitcast.94, f32[512,512]{1,0:T(8,128)} %copy.30, f32[]{:T(128)} %constant.39.clone.1), kind=kCustom, calls=%fused_computation.49 | custom fusion | flops 262144 | bytes 1049088 | tf_op jit(solution)/shard_map/scatter-add | solution.py:60
  77.4 6.0 %reduce-scatter.3.cloned.1.call-done = bf16[256,512]{1,0:T(8,128)(2,1)} async-done(((bf16[512,512]{1,0:T(8,128)(2,1)}), bf16[256,512]{1,0:T(8,128)(2,1)}) %reduce-scatter.3.cloned.1.call-update) | async-done | bytes 262160 | tf_op jit(solution)/shard_map/reduce_scatter | solution.py:49
  87.2 5.6 %all-to-all-start.2 = ((bf16[16,32,512]{2,1,0:T(8,128)(2,1)}), bf16[16,32,512]{2,1,0:T(8,128)(2,1)S(1)}, u32[]{:S(2)}, u32[]{:S(2)}) async-start(bf16[16,32,512]{2,1,0:T(8,128)(2,1)} %bitcast.74), calls=%async_computation.3 | async-start | bytes 1048576 | tf_op jit(solution)/shard_map/all_to_all | solution.py:92
  92.9 14.1 %all-to-all-done.2 = bf16[16,32,512]{2,1,0:T(8,128)(2,1)S(1)} async-done(((bf16[16,32,512]{2,1,0:T(8,128)(2,1)}), bf16[16,32,512]{2,1,0:T(8,128)(2,1)S(1)}, u32[]{:S(2)}, u32[]{:S(2)}) %all-to-all-start.2) | async-done | bytes 524320 | tf_op jit(solution)/shard_map/all_to_all | solution.py:92
  108.6 4.2 all-to-all-start.3
  116.4 10.8 %all-to-all-done.3 = bf16[16,32,512]{2,1,0:T(8,128)(2,1)} async-done(((bf16[16,32,512]{2,1,0:T(8,128)(2,1)}), bf16[16,32,512]{2,1,0:T(8,128)(2,1)}, u32[]{:S(2)}, u32[]{:S(2)}) %all-to-all-start.3) | async-done | bytes 524320 | tf_op jit(solution)/shard_map/all_to_all | solution.py:99
  128.3 4.8 %scatter_fusion = f32[512,512]{1,0:T(8,128)S(1)} fusion(f32[512,512]{1,0:T(8,128)S(1)} %bitcast_convert_fusion.1, s32[512]{0:T(512)S(1)} %bitcast.86, f32[512,512]{1,0:T(8,128)} %fusion.28), kind=kCustom, calls=%fused_computation.12 | custom fusion | flops 262144 | bytes 3147776 | tf_op jit(solution)/shard_map/scatter-add | solution.py:111
  134.4 4.2 all-to-all-start.4
  138.6 14.2 %all-to-all-done.4 = bf16[16,32,512]{2,1,0:T(8,128)(2,1)S(1)} async-done(((bf16[16,32,512]{2,1,0:T(8,128)(2,1)}), bf16[16,32,512]{2,1,0:T(8,128)(2,1)S(1)}, u32[]{:S(2)}, u32[]{:S(2)}) %all-to-all-start.4) | async-done | bytes 524320 | tf_op jit(solution)/shard_map/all_to_all | solution.py:83
  163.0 9.7 %all-to-all-done.5 = bf16[16,32,512]{2,1,0:T(8,128)(2,1)S(1)} async-done(((bf16[16,32,512]{2,1,0:T(8,128)(2,1)}), bf16[16,32,512]{2,1,0:T(8,128)(2,1)S(1)}, u32[]{:S(2)}, u32[]{:S(2)}) %all-to-all-start.5) | async-done | bytes 524320 | tf_op jit(solution)/shard_map/all_to_all | solution.py:86
  177.0 9.0 %all_gather.13 = bf16[512,512]{1,0:T(8,128)(2,1)S(1)} all-gather(bf16[256,512]{1,0:T(8,128)(2,1)S(1)} %broadcast_select_fusion.6), channel_id=1, replica_groups=mesh['wide'=16,'narrow'=2] {'narrow'}, dimensions={0}, use_global_device_ids=true | all-gather | bytes 786432 | tf_op jit(solution)/shard_map/all_gather | solution.py:34
  200.4 4.5 %scatter_custom_fusion.3 = f32[512,512]{1,0:T(8,128)S(1)} fusion(s32[512]{0:T(512)S(1)} %bitcast.93, f32[512,512]{1,0:T(8,128)} %copy.34, f32[]{:T(128)} %constant.39.clone.1), kind=kCustom, calls=%fused_computation.47 | custom fusion | flops 262144 | bytes 1049088 | tf_op jit(solution)/shard_map/scatter-add | solution.py:60
  208.7 4.8 %all-to-all-start.6 = ((bf16[16,32,512]{2,1,0:T(8,128)(2,1)}), bf16[16,32,512]{2,1,0:T(8,128)(2,1)S(1)}, u32[]{:S(2)}, u32[]{:S(2)}) async-start(bf16[16,32,512]{2,1,0:T(8,128)(2,1)} %bitcast.26), calls=%async_computation.8 | async-start | bytes 1048576 | tf_op jit(solution)/shard_map/all_to_all | solution.py:92
  213.7 20.3 %all-to-all-done.6 = bf16[16,32,512]{2,1,0:T(8,128)(2,1)S(1)} async-done(((bf16[16,32,512]{2,1,0:T(8,128)(2,1)}), bf16[16,32,512]{2,1,0:T(8,128)(2,1)S(1)}, u32[]{:S(2)}, u32[]{:S(2)}) %all-to-all-start.6) | async-done | bytes 524320 | tf_op jit(solution)/shard_map/all_to_all | solution.py:92
  235.5 11.3 %all-to-all-start.7 = ((bf16[16,32,512]{2,1,0:T(8,128)(2,1)}), bf16[16,32,512]{2,1,0:T(8,128)(2,1)S(1)}, u32[]{:S(2)}, u32[]{:S(2)}) async-start(bf16[16,32,512]{2,1,0:T(8,128)(2,1)} %select_convert_fusion), calls=%async_computation.9 | async-start | bytes 1048576 | tf_op jit(solution)/shard_map/all_to_all | solution.py:99
  251.3 9.8 %all-to-all-done.7 = bf16[16,32,512]{2,1,0:T(8,128)(2,1)S(1)} async-done(((bf16[16,32,512]{2,1,0:T(8,128)(2,1)}), bf16[16,32,512]{2,1,0:T(8,128)(2,1)S(1)}, u32[]{:S(2)}, u32[]{:S(2)}) %all-to-all-start.7) | async-done | bytes 524320 | tf_op jit(solution)/shard_map/all_to_all | solution.py:99
  261.3 4.7 %scatter_fusion.1 = f32[512,512]{1,0:T(8,128)S(1)} fusion(f32[512,512]{1,0:T(8,128)S(1)} %bitcast_convert_fusion, s32[512]{0:T(512)S(1)} %bitcast.85, f32[512,512]{1,0:T(8,128)} %fusion.29), kind=kCustom, calls=%fused_computation.15 | custom fusion | flops 262144 | bytes 3147776 | tf_op jit(solution)/shard_map/scatter-add | solution.py:111
  269.3 144.3 %all-gather.3.cloned.1.call-done = f32[16384,512]{1,0:T(8,128)} async-done(((f32[512,512]{1,0:T(8,128)}), f32[16384,512]{1,0:T(8,128)}) %all-gather.3.cloned.1.call-update) | async-done | bytes 33554448 | tf_op jit(solution)/shard_map/all_gather | solution.py:120
  413.6 13.2 %reduce_sum.97 = f32[512,512]{1,0:T(8,128)} reduce(f32[32,512,512]{2,1,0:T(8,128)} %bitcast.73, f32[]{:T(128)} %constant.39.clone.1), dimensions={0}, to_apply=%region_16.21 | reduce | flops 8126464 | bytes 34603012 | tf_op jit(solution)/shard_map/reduce_sum | solution.py:120
  (121 shorter events, 78.1 us)
Async XLA Ops:
  7.2 57.0 %copy-start = (bf16[512,512]{1,0:T(8,128)(2,1)S(1)}, bf16[512,512]{1,0:T(8,128)(2,1)}, u32[]{:S(2)}) copy-start(bf16[512,512]{1,0:T(8,128)(2,1)} %param.18) | copy-start | bytes 1572868
  7.2 85.6 %copy-start.11 = (s32[2,16]{1,0:T(2,128)S(1)}, s32[2,16]{1,0:T(2,128)}, u32[]{:S(2)}) copy-start(s32[2,16]{1,0:T(2,128)} %param.22) | copy-start | bytes 388
  7.2 105.6 %copy-start.9 = (s32[2,512]{1,0:T(2,128)S(1)}, s32[2,512]{1,0:T(2,128)}, u32[]{:S(2)}) copy-start(s32[2,512]{1,0:T(2,128)} %param.19) | copy-start | bytes 12292
  9.3 21.7 %all-to-all-start = ((bf16[16,32,512]{2,1,0:T(8,128)(2,1)}), bf16[16,32,512]{2,1,0:T(8,128)(2,1)S(1)}, u32[]{:S(2)}, u32[]{:S(2)}) async-start(bf16[16,32,512]{2,1,0:T(8,128)(2,1)} %bitcast.6), calls=%async_computation | async-start | bytes 1048576 | tf_op jit(solution)/shard_map/all_to_all | solution.py:83
  18.3 115.0 %copy-start.10 = (f32[512]{0:T(512)S(1)}, f32[512]{0:T(512)}, u32[]{:S(2)}) copy-start(f32[512]{0:T(512)} %param.17) | copy-start | bytes 6148
  18.3 115.0 %copy-start.1 = (f32[512,512]{1,0:T(8,128)S(1)}, f32[512,512]{1,0:T(8,128)}, u32[]{:S(2)}) copy-start(f32[512,512]{1,0:T(8,128)} %param.16) | copy-start | bytes 3145732
  32.5 18.4 %all-to-all-start.1 = ((bf16[16,32,512]{2,1,0:T(8,128)(2,1)}), bf16[16,32,512]{2,1,0:T(8,128)(2,1)S(1)}, u32[]{:S(2)}, u32[]{:S(2)}) async-start(bf16[16,32,512]{2,1,0:T(8,128)(2,1)} %broadcast_select_fusion.2), calls=%async_computation.1 | async-start | bytes 1048576 | tf_op jit(solution)/shard_map/all_to_all | solution.py:86
  36.7 46.7 %reduce-scatter.3.cloned.1.call-start = ((), (), s32[]{:S(2)}) async-start(), calls=%async_computation.10 | async-start | bytes 786432 | tf_op jit(solution)/shard_map/reduce_scatter | solution.py:49
  64.2 6.1 %copy-start.2 = (bf16[512,512]{1,0:T(8,128)(2,1)}, bf16[512,512]{1,0:T(8,128)(2,1)S(1)}, u32[]{:S(2)}) copy-start(bf16[512,512]{1,0:T(8,128)(2,1)S(1)} %all_gather.12) | copy-start | bytes 1572868
  66.1 4.3 copy-start.4
  66.5 1.0 copy-start.7
  87.2 19.9 %all-to-all-start.2 = ((bf16[16,32,512]{2,1,0:T(8,128)(2,1)}), bf16[16,32,512]{2,1,0:T(8,128)(2,1)S(1)}, u32[]{:S(2)}, u32[]{:S(2)}) async-start(bf16[16,32,512]{2,1,0:T(8,128)(2,1)} %bitcast.74), calls=%async_computation.3 | async-start | bytes 1048576 | tf_op jit(solution)/shard_map/all_to_all | solution.py:92
  108.6 18.5 %all-to-all-start.3 = ((bf16[16,32,512]{2,1,0:T(8,128)(2,1)}), bf16[16,32,512]{2,1,0:T(8,128)(2,1)}, u32[]{:S(2)}, u32[]{:S(2)}) async-start(bf16[16,32,512]{2,1,0:T(8,128)(2,1)} %select_convert_fusion.1), calls=%async_computation.4 | async-start | bytes 1048576 | tf_op jit(solution)/shard_map/all_to_all | solution.py:99
  114.9 1.5 copy-start.5
  134.4 18.4 %all-to-all-start.4 = ((bf16[16,32,512]{2,1,0:T(8,128)(2,1)}), bf16[16,32,512]{2,1,0:T(8,128)(2,1)S(1)}, u32[]{:S(2)}, u32[]{:S(2)}) async-start(bf16[16,32,512]{2,1,0:T(8,128)(2,1)} %bitcast.21), calls=%async_computation.5 | async-start | bytes 1048576 | tf_op jit(solution)/shard_map/all_to_all | solution.py:83
  154.3 18.4 %all-to-all-start.5 = ((bf16[16,32,512]{2,1,0:T(8,128)(2,1)}), bf16[16,32,512]{2,1,0:T(8,128)(2,1)S(1)}, u32[]{:S(2)}, u32[]{:S(2)}) async-start(bf16[16,32,512]{2,1,0:T(8,128)(2,1)} %broadcast_select_fusion), calls=%async_computation.6 | async-start | bytes 1048576 | tf_op jit(solution)/shard_map/all_to_all | solution.py:86
  158.5 46.5 %reduce-scatter.5.cloned.1.call-start = ((), (), s32[]{:S(2)}) async-start(), calls=%async_computation.11 | async-start | bytes 786432 | tf_op jit(solution)/shard_map/reduce_scatter | solution.py:49
  187.8 0.8 copy-start.3
  188.3 1.0 copy-start.8
  190.6 223.0 %all-gather.3.cloned.1.call-start = ((), (), s32[]{:S(2)}) async-start(), calls=%async_computation.12 | async-start | bytes 34603008 | tf_op jit(solution)/shard_map/all_gather | solution.py:120
  194.4 0.8 copy-start.6
  208.7 25.3 %all-to-all-start.6 = ((bf16[16,32,512]{2,1,0:T(8,128)(2,1)}), bf16[16,32,512]{2,1,0:T(8,128)(2,1)S(1)}, u32[]{:S(2)}, u32[]{:S(2)}) async-start(bf16[16,32,512]{2,1,0:T(8,128)(2,1)} %bitcast.26), calls=%async_computation.8 | async-start | bytes 1048576 | tf_op jit(solution)/shard_map/all_to_all | solution.py:92
  235.5 25.6 %all-to-all-start.7 = ((bf16[16,32,512]{2,1,0:T(8,128)(2,1)}), bf16[16,32,512]{2,1,0:T(8,128)(2,1)S(1)}, u32[]{:S(2)}, u32[]{:S(2)}) async-start(bf16[16,32,512]{2,1,0:T(8,128)(2,1)} %select_convert_fusion), calls=%async_computation.9 | async-start | bytes 1048576 | tf_op jit(solution)/shard_map/all_to_all | solution.py:99
Sparse Core Ops, SparseCore 0:
  68.9 14.3 reduce-scatter.2
  190.7 13.4 reduce-scatter.4
  207.3 206.2 all-gather.2
